TPU v7x, 32 devices: a whole 2x2x4 slice. The times are simulated.
32 devices in a mesh: dp: 8 (over y, x, core), hid: 4 (over z).
Axes of the slice: x: 2, y: 2, z: 4, core: 2. Of those that a mesh axis runs over, the one named last changes fastest.
Arguments:
- tokens: bfloat16 [4096, 8192], P('dp', 'hid'), may hold values from -6 to 6
- up_blocks: bfloat16 [7, 64, 128, 1024], P(None, 'hid', 'dp'), may hold values from -0.1875 to 0.1875
- up_left: bfloat16 [8192, 512], P('hid'), may hold values from -0.0625 to 0.0625
- up_right: bfloat16 [512, 65536], P(None, 'hid'), may hold values from -0.25 to 0.25
- down_blocks: bfloat16 [7, 64, 1024, 128], P(None, 'hid', 'dp'), may hold values from -0.0625 to 0.0625
- down_left: bfloat16 [65536, 512], P('hid'), may hold values from -0.0234375 to 0.0234375
- down_right: bfloat16 [512, 8192], P(None, 'hid'), may hold values from -0.25 to 0.25
Outputs:
- mixed: bfloat16 [4096, 8192], P('dp', 'hid')
All inputs are finite; a program needn't handle non-finite values.
Results may differ from a plain program's by a relative error of at most 0.0059.
Values may be sent and summed in bfloat16 or wider, within the bound.
A program may use at most 384 MiB of HBM per device.

v0:
```python
import jax
import jax.numpy as jnp
from jax import lax
from jax.sharding import PartitionSpec as P


def from_partner(block, axis, stride):
    count = lax.axis_size(axis)
    route = []
    for low in range(count):
        high = low | 1 << stride
        if high != low and high < count:
            route += [(low, high), (high, low)]
    return lax.ppermute(block, axis, route)


def swap_blocks(values, block_span, along_axis):
    full_shape = values.shape
    extent = full_shape[along_axis]
    split_shape = (
        full_shape[:along_axis]
        + (extent // (2 * block_span), 2, block_span)
        + full_shape[along_axis + 1 :]
    )
    return jnp.flip(values.reshape(split_shape), along_axis + 1).reshape(full_shape)


def shards(tokens, up_blocks, up_left, up_right, down_blocks, down_left, down_right):
    token_rows = tokens.shape[0]
    local_blocks = up_blocks.shape[1]
    block_size = down_blocks.shape[3]
    term_count = up_blocks.shape[0]
    pieces = tokens.reshape(token_rows, local_blocks, block_size)
    sources = []
    for step_index in range(term_count):
        block_span = 0 if step_index == 0 else 2 ** (step_index - 1)
        if block_span == 0:
            sources.append(pieces)
        elif block_span < local_blocks:
            sources.append(swap_blocks(pieces, block_span, 1))
        else:
            swap_bit = (block_span // local_blocks).bit_length() - 1
            partner_rows = from_partner(tokens, "hid", swap_bit)
            sources.append(partner_rows.reshape(token_rows, local_blocks, block_size))
    stacked = jnp.stack(sources)
    up_full = lax.all_gather(up_blocks, "dp", axis=2, tiled=True)
    hidden_sum = jnp.einsum("tabk,tbkn->abn", stacked, up_full, preferred_element_type=jnp.float32)
    down_full = lax.all_gather(down_blocks, "dp", axis=2, tiled=True)
    rank_up = lax.psum(jnp.dot(tokens, up_left, preferred_element_type=jnp.float32), "hid").astype(
        jnp.bfloat16
    )
    pre_activation = hidden_sum.reshape(
        token_rows, hidden_sum.shape[1] * hidden_sum.shape[2]
    ) + jnp.dot(rank_up, up_right, preferred_element_type=jnp.float32)
    active = jax.nn.gelu(pre_activation, approximate=False).astype(jnp.bfloat16)
    grouped = active.reshape(token_rows, local_blocks, hidden_sum.shape[2])
    contributions = jnp.einsum(
        "abn,tbnk->tabk", grouped, down_full, preferred_element_type=jnp.float32
    )
    out_sum = jnp.zeros((token_rows, local_blocks, block_size), jnp.float32)
    for step_index in range(term_count):
        block_span = 0 if step_index == 0 else 2 ** (step_index - 1)
        if block_span == 0:
            out_sum = contributions[0]
        elif block_span < local_blocks:
            out_sum = out_sum + swap_blocks(contributions[step_index], block_span, 1)
        else:
            swap_bit = (block_span // local_blocks).bit_length() - 1
            out_sum = out_sum + from_partner(contributions[step_index], "hid", swap_bit)
    rank_down = lax.psum(
        jnp.dot(active, down_left, preferred_element_type=jnp.float32), "hid"
    ).astype(jnp.bfloat16)
    result = out_sum.reshape(token_rows, local_blocks * block_size) + jnp.dot(
        rank_down, down_right, preferred_element_type=jnp.float32
    )
    return result.astype(jnp.bfloat16)


def solution(mesh):
    placed = (
        P("dp", "hid"),
        P(None, "hid", "dp", None),
        P("hid", None),
        P(None, "hid"),
        P(None, "hid", "dp", None),
        P("hid", None),
        P(None, "hid"),
    )
    return jax.shard_map(
        shards, mesh=mesh, in_specs=placed, out_specs=P("dp", "hid"), check_vma=False
    )
```

profile of v0, /device:TPU:0, one launch (start us, length us, event | category | flops | bytes accessed | tf_op | source)
XLA Modules:
  0.0 731.4 jit_solution(11911932797676576701)
XLA Ops:
  6.5 0.0 copy-start
  6.5 0.0 all-gather.3.cloned.1.call-start
  6.5 4.7 copy.28
  11.2 0.0 all-gather.3.cloned.1.call-update
  11.2 0.0 all-gather.5.cloned.1.call-start
  11.3 6.1 copy.31
  17.4 0.0 all-gather.5.cloned.1.call-update
  17.4 3.9 copy.18
  21.3 3.1 collective-permute-start
  24.4 2.6 collective-permute-start.1
  27.0 4.6 reshape_reshape.12
  31.6 4.5 reshape_reshape.13
  36.0 4.5 reshape_reshape.14
  40.5 3.9 copy.25
  44.4 3.4 copy.19
  47.8 3.1 rev.32
  51.0 3.4 copy.20
  54.4 3.2 rev.33
  57.6 3.4 copy.21
  61.0 3.1 rev.34
  64.1 2.2 copy.42
  66.3 1.9 copy.22
  68.2 3.1 rev.35
  71.4 4.2 fusion.25
  75.5 5.2 constant_dynamic-update-slice_fusion.6
  80.8 3.4 constant_dynamic-update-slice_fusion.5
  84.2 0.0 copy-done.2
  84.2 1.7 constant_dynamic-update-slice_fusion.4
  85.9 0.0 copy-done.3
  85.9 1.7 constant_dynamic-update-slice_fusion.3
  87.6 0.0 copy-done.4
  87.6 1.7 constant_dynamic-update-slice_fusion.2
  89.3 65.1 %all-reduce.2 = bf16[512,512]{1,0:T(8,128)(2,1)} all-reduce(f32[512,512]{1,0:T(8,128)S(1)} %fusion.25), channel_id=1, replica_groups=mesh['dp'=8,'hid'=4] {'hid'}, use_global_device_ids=true, to_apply=%region_0.1 | all-reduce | flops 262144 | bytes 1572864 | tf_op jit(solution)/shard_map/psum | solution.py:49
  154.3 0.0 collective-permute-done
  154.3 4.1 copy.26
  158.5 0.0 collective-permute-done.1
  158.5 3.9 copy.27
  162.4 3.4 constant_dynamic-update-slice_fusion.1
  165.8 3.9 constant_dynamic-update-slice_fusion
  169.7 31.9 %convolution_bitcast_fusion = f32[512,16,1024]{2,0,1:T(8,128)} fusion(bf16[7,512,16,128]{3,1,0,2:T(8,128)(2,1)} %constant_dynamic-update-slice_fusion, bf16[7,16,128,1024]{3,2,0,1:T(8,128)(2,1)} %all-gather.3.cloned.1.call-done), kind=kOutput, calls=%fused_computation.21 | convolution fusion | flops 15032385536 | bytes 77594624 | tf_op jit(solution)/shard_map/tabk,tbkn->abn/dot_general | solution.py:47
  201.6 32.2 %copy.29 = f32[512,16,1024]{0,2,1:T(8,128)} copy(f32[512,16,1024]{2,0,1:T(8,128)} %convolution_bitcast_fusion) | data formatting | bytes 67108864 | tf_op jit(solution)/shard_map/tabk,tbkn->abn/transpose | solution.py:47
  233.8 31.3 %copy.30 = f32[512,16384]{1,0:T(8,128)} copy(f32[512,16384]{0,1:T(8,128)} %bitcast.69) | data formatting | bytes 67108864 | tf_op jit(solution)/shard_map/reshape | solution.py:52
  265.1 0.0 copy-done.5
  265.1 82.0 %fusion.2 = bf16[512,16384]{1,0:T(8,128)(2,1)S(1)} fusion(f32[512,16384]{1,0:T(8,128)} %copy.30, bf16[512,16384]{1,0:T(8,128)(2,1)} %param.10, bf16[512,512]{1,0:T(8,128)(2,1)S(1)} %copy-done.5), kind=kOutput, calls=%fused_computation.3 | convolution fusion | flops 9143582720 | bytes 67633152 | tf_op jit(solution)/shard_map/dot_general | solution.py:54
  347.1 0.0 copy-start.1
  347.1 5.7 copy-done.1
  352.8 12.0 %copy.43 = bf16[64,8,16,1024]{3,2,1,0:T(8,128)(2,1)} copy(bf16[64,8,16,1024]{3,1,2,0:T(8,128)(2,1)S(1)} %bitcast.75) | data formatting | bytes 33554432
  364.8 91.7 %fusion.12 = f32[7,512,16,128]{1,3,0,2:T(8,128)} fusion(bf16[7,16,1024,128]{2,3,0,1:T(8,128)(2,1)} %all-gather.5.cloned.1.call-done, bf16[512,16,1024,1]{2,1,0,3:T(8,128)(2,1)} %bitcast.76), kind=kOutput, calls=%fused_computation.22 | convolution fusion | flops 15032385536 | bytes 75497472 | tf_op jit(solution)/shard_map/abn,tbnk->tabk/dot_general | solution.py:57
  456.6 17.7 %fusion.24 = (f32[1,512,16,128]{1,3,0,2:T(8,128)}, f32[512,16,128]{0,2,1:T(8,128)}, f32[1,512,16,128]{1,3,0,2:T(8,128)}, f32[1,512,16,128]{1,3,0,2:T(8,128)}, f3...) fusion(f32[7,512,16,128]{1,3,0,2:T(8,128)} %fusion.12), kind=kLoop, calls=%fused_computation.43 | loop fusion | bytes 50331648 | tf_op jit(solution)/shard_map/slice | solution.py:66
  474.3 0.2 collective-permute-start.2
  474.5 2.4 collective-permute-start.3
  476.9 4.8 rev.36
  481.7 4.7 rev.37
  486.4 4.7 rev.38
  491.2 4.8 rev.39
  496.0 18.1 %fusion.26 = f32[512,512]{1,0:T(8,128)} fusion(bf16[512,16384]{1,0:T(8,128)(2,1)} %copy-done.1, bf16[16384,512]{1,0:T(8,128)(2,1)} %param.12), kind=kOutput, calls=%fused_computation.45 | convolution fusion | flops 8589934592 | bytes 34603008 | tf_op jit(solution)/shard_map/dot_general | solution.py:71
  514.1 183.0 %all-reduce.3 = bf16[512,512]{1,0:T(8,128)(2,1)S(1)} all-reduce(f32[512,512]{1,0:T(8,128)} %fusion.26), channel_id=1, replica_groups=mesh['dp'=8,'hid'=4] {'hid'}, use_global_device_ids=true, to_apply=%region_1.2 | all-reduce | flops 262144 | bytes 1572864 | tf_op jit(solution)/shard_map/psum | solution.py:70
  697.0 0.0 copy-done
  697.0 3.2 fusion.27
  700.2 0.0 collective-permute-done.2
  700.2 0.0 collective-permute-done.3
  700.2 13.4 %fusion.20 = f32[512,16,128]{0,2,1:T(8,128)} fusion(f32[512,16,128]{0,2,1:T(8,128)} %collective-permute-done.3, f32[512,16,128]{0,2,1:T(8,128)} %collective-permute-done.2, f32[7,512,16,128]{1,3,0,2:T(8,128)} %fusion.12, f32[512,1,2,8,128]{0,4,3,2,1:T(8,128)} %rev.39, f32[512,2,2,4,128]{0,4,3,2,1:T(8,128)} %rev.38, f32[512,4,2,2,128]{0,4,3,2,1:T(8,128)} %rev.37, ...), kind=kLoop, calls=%fused_computation.31 | loop fusion | flops 6291456 | bytes 33554432 | tf_op jit(solution)/shard_map/add | solution.py:69
  713.6 5.4 copy.35
  719.0 5.4 add_convert_fusion
  (6 shorter events, 0.0 us)
Async XLA Ops:
  6.5 690.5 %copy-start = (bf16[512,2048]{1,0:T(8,128)(2,1)S(1)}, bf16[512,2048]{1,0:T(8,128)(2,1)}, u32[]{:S(2)}) copy-start(bf16[512,2048]{1,0:T(8,128)(2,1)} %param.13) | copy-start | bytes 6291460
  6.5 163.1 %all-gather.3.cloned.1.call-start = ((), (), s32[]{:S(2)}) async-start(), calls=%async_computation | async-start | bytes 33030144 | tf_op jit(solution)/shard_map/all_gather | solution.py:46
  11.2 353.6 %all-gather.5.cloned.1.call-start = ((), (), s32[]{:S(2)}) async-start(), calls=%async_computation.1 | async-start | bytes 33030144 | tf_op jit(solution)/shard_map/all_gather | solution.py:48
  21.3 133.0 %collective-permute-start = (bf16[512,2048]{0,1:T(8,128)(2,1)}, bf16[512,2048]{0,1:T(8,128)(2,1)}, u32[]{:S(2)}, u32[]{:S(2)}) collective-permute-start(bf16[512,2048]{0,1:T(8,128)(2,1)} %copy.18), channel_id=1, source_target_pairs={{0,1},{1,0},{2,3},{3,2},{4,5},{5,4},{6,7},{7,6},{8,9},{9,8},{10,11... | collective-permute-start | bytes 6291464 | tf_op jit(solution)/shard_map/ppermute | solution.py:14
  24.4 134.1 %collective-permute-start.1 = (bf16[512,2048]{0,1:T(8,128)(2,1)}, bf16[512,2048]{0,1:T(8,128)(2,1)}, u32[]{:S(2)}, u32[]{:S(2)}) collective-permute-start(bf16[512,2048]{0,1:T(8,128)(2,1)} %copy.18), channel_id=1, source_target_pairs={{0,2},{2,0},{1,3},{3,1},{4,6},{6,4},{5,7},{7,5},{8,10},{10,8},{9,1... | collective-permute-start | bytes 6291464 | tf_op jit(solution)/shard_map/ppermute | solution.py:14
  71.3 12.8 %copy-start.2 = (bf16[512,4,2,2,128]{4,0,3,2,1:T(8,128)(2,1)S(1)}, bf16[512,4,2,2,128]{4,0,3,2,1:T(8,128)(2,1)}, u32[]{:S(2)}) copy-start(bf16[512,4,2,2,128]{4,0,3,2,1:T(8,128)(2,1)} %rev.33) | copy-start | bytes 6291460
  71.4 14.5 %copy-start.3 = (bf16[512,2,2,4,128]{4,0,3,2,1:T(8,128)(2,1)S(1)}, bf16[512,2,2,4,128]{4,0,3,2,1:T(8,128)(2,1)}, u32[]{:S(2)}) copy-start(bf16[512,2,2,4,128]{4,0,3,2,1:T(8,128)(2,1)} %rev.34) | copy-start | bytes 6291460
  71.4 16.2 %copy-start.4 = (bf16[512,1,2,8,128]{4,0,3,2,1:T(8,128)(2,1)S(1)}, bf16[512,1,2,8,128]{4,0,3,2,1:T(8,128)(2,1)}, u32[]{:S(2)}) copy-start(bf16[512,1,2,8,128]{4,0,3,2,1:T(8,128)(2,1)} %rev.35) | copy-start | bytes 6291460
  233.8 31.3 %copy-start.5 = (bf16[512,512]{1,0:T(8,128)(2,1)S(1)}, bf16[512,512]{1,0:T(8,128)(2,1)}, u32[]{:S(2)}) copy-start(bf16[512,512]{1,0:T(8,128)(2,1)} %all-reduce.2) | copy-start | bytes 1572868
  347.1 5.7 copy-start.1
  474.3 226.0 %collective-permute-start.2 = (f32[512,16,128]{0,2,1:T(8,128)}, f32[512,16,128]{0,2,1:T(8,128)}, u32[]{:S(2)}, u32[]{:S(2)}) collective-permute-start(f32[512,16,128]{0,2,1:T(8,128)} %get-tuple-element.10), channel_id=1, source_target_pairs={{0,1},{1,0},{2,3},{3,2},{4,5},{5,4},{6,7},{7,6},{8,9},{9,8},{10,11... | collective-permute-start | bytes 12582920 | tf_op jit(solution)/shard_map/ppermute | solution.py:14
  474.5 225.7 %collective-permute-start.3 = (f32[512,16,128]{0,2,1:T(8,128)}, f32[512,16,128]{0,2,1:T(8,128)}, u32[]{:S(2)}, u32[]{:S(2)}) collective-permute-start(f32[512,16,128]{0,2,1:T(8,128)} %get-tuple-element.6), channel_id=1, source_target_pairs={{0,2},{2,0},{1,3},{3,1},{4,6},{6,4},{5,7},{7,5},{8,10},{10,8},{9,1... | collective-permute-start | bytes 12582920 | tf_op jit(solution)/shard_map/ppermute | solution.py:14
Sparse Core Ops, SparseCore 0:
  11.3 145.7 all-gather.2
  159.0 148.8 all-gather.4
where the time goes:
time: 740 us; the launch traced here: 731 us
  blocking collectives  248 us (34%)
  matrix products  231 us (31%)
  local copies, waits for them, and re-layouts  211 us (29%)
  other arithmetic  18.8 us (3%)
  between operations  13.7 us (2%)
  starting transfers between devices  8.36 us (1%)
    psum x1, blocking collectives, shards(): lax.psum(jnp.dot(active, down_left, preferred_element_type=jnp.float32),...  183 us
    dot_general x1, matrix products, shards(): jnp.einsum('abn,tbnk->tabk', grouped, down_full, preferred_element_type=j...  91.7 us
    dot_general x1, matrix products, shards(): jnp.dot(rank_up, up_right, preferred_element_type=jnp.float32)  82 us
    psum x1, blocking collectives, shards(): lax.psum(jnp.dot(tokens, up_left, preferred_element_type=jnp.float32), 'h...  65.1 us
    unnamed x23, local copies, waits for them, and re-layouts  51.8 us
    transpose x1, local copies, waits for them, and re-layouts, shards(): jnp.einsum('tabk,tbkn->abn', stacked, up_full, preferred_element_type=jnp...  32.2 us
    dot_general x1, matrix products, shards(): jnp.einsum('tabk,tbkn->abn', stacked, up_full, preferred_element_type=jnp...  31.9 us
    rev x8, local copies, waits for them, and re-layouts, swap_blocks(): jnp.flip(values.reshape(split_shape), along_axis + 1).reshape(full_shape)  31.6 us
  transfers between devices with their start and end apart: 6, of which 0 were waited for; matrix products, arithmetic and copies ran while one was open for 43% of the time, Pallas kernels for 0%

commit v1 on v0

--- a/solution.py
+++ b/solution.py
@@ -2,6 +2,11 @@
 import jax.numpy as jnp
 from jax import lax
 from jax.sharding import PartitionSpec as P
+
+
+def add_all(array, axis):
+    blocks = lax.all_gather(array, axis)
+    return jnp.sum(blocks, axis=0)
 
 
 def from_partner(block, axis, stride):
@@ -46,7 +51,7 @@
     up_full = lax.all_gather(up_blocks, "dp", axis=2, tiled=True)
     hidden_sum = jnp.einsum("tabk,tbkn->abn", stacked, up_full, preferred_element_type=jnp.float32)
     down_full = lax.all_gather(down_blocks, "dp", axis=2, tiled=True)
-    rank_up = lax.psum(jnp.dot(tokens, up_left, preferred_element_type=jnp.float32), "hid").astype(
+    rank_up = add_all(jnp.dot(tokens, up_left, preferred_element_type=jnp.float32), "hid").astype(
         jnp.bfloat16
     )
     pre_activation = hidden_sum.reshape(

time: 740 us -> 900 us (1.22)
  waiting for transfers between devices: 0.05 us -> 206 us
  blocking collectives: 248 us -> 182 us
  local copies, waits for them, and re-layouts: 211 us -> 225 us
    all_gather x1, waiting for transfers between devices: 0.01 us -> 113 us  [shards(): up_full = lax.all_gather(up_blocks, 'dp', axis=2, tiled=True)]
    ppermute x4, waiting for transfers between devices: 0.01 us -> 93.3 us  [from_partner(): return lax.ppermute(block, axis, route)]
    psum x1 -> x0, blocking collectives: 65.1 us -> none  [shards(): lax.psum(jnp.dot(tokens, up_left, preferred_element_type=jnp.float32), 'h...]
    reshape x1, local copies, waits for them, and re-layouts: 31.3 us -> 45.3 us  [shards(): hidden_sum.reshape(token_rows, hidden_sum.shape[1] * hidden_sum.shape[2])]
    unnamed x23 -> x19, local copies, waits for them, and re-layouts: 51.8 us -> 51.2 us
  transfers between devices with their start and end apart: 6 -> 7, of which waited for: 0 -> 2; matrix products, arithmetic and copies ran while one was open for 43% -> 37% of each run, Pallas kernels for 0% -> 0%
where the time goes in v1:
time: 900 us; the launch traced here: 888 us
  matrix products  231 us (26%)
  local copies, waits for them, and re-layouts  225 us (25%)
  waiting for transfers between devices  206 us (23%)
  blocking collectives  182 us (20%)
  other arithmetic  21.5 us (2%)
  between operations  13.6 us (2%)
  starting transfers between devices  9.33 us (1%)
    psum x1, blocking collectives, shards(): lax.psum(jnp.dot(active, down_left, preferred_element_type=jnp.float32),...  182 us
    all_gather x1, waiting for transfers between devices, shards(): up_full = lax.all_gather(up_blocks, 'dp', axis=2, tiled=True)  113 us
    ppermute x4, waiting for transfers between devices, from_partner(): return lax.ppermute(block, axis, route)  93.3 us
    dot_general x1, matrix products, shards(): jnp.einsum('abn,tbnk->tabk', grouped, down_full, preferred_element_type=j...  91.5 us
    dot_general x1, matrix products, shards(): jnp.dot(rank_up, up_right, preferred_element_type=jnp.float32)  82 us
    unnamed x19, local copies, waits for them, and re-layouts  51.2 us
    reshape x1, local copies, waits for them, and re-layouts, shards(): hidden_sum.reshape(token_rows, hidden_sum.shape[1] * hidden_sum.shape[2])  45.3 us
    transpose x1, local copies, waits for them, and re-layouts, shards(): jnp.einsum('tabk,tbkn->abn', stacked, up_full, preferred_element_type=jnp...  32.4 us
  transfers between devices with their start and end apart: 7, of which 2 were waited for; matrix products, arithmetic and copies ran while one was open for 37% of the time, Pallas kernels for 0%

profile of v1, /device:TPU:0, one launch (start us, length us, event | category | flops | bytes accessed | tf_op | source)
XLA Modules:
  0.0 888.3 jit_solution(6299470307812568661)
XLA Ops:
  6.5 0.0 copy-start
  6.5 0.0 all-gather.9.cloned.1.call-start
  6.5 4.6 fusion.25
  11.1 0.0 all-gather.9.cloned.1.call-update
  11.2 0.0 all-gather.5.cloned.1.call-start
  11.2 4.5 copy.28
  15.8 0.0 all-gather.5.cloned.1.call-update
  15.8 0.0 all-gather.7.cloned.1.call-start
  15.8 6.1 copy.31
  21.9 0.0 all-gather.7.cloned.1.call-update
  22.0 4.0 copy.18
  26.0 3.0 collective-permute-start
  29.0 2.6 collective-permute-start.1
  31.6 4.5 reshape_reshape.12
  36.1 4.4 reshape_reshape.13
  40.5 4.5 reshape_reshape.14
  45.0 3.9 copy.25
  48.9 3.5 copy.19
  52.3 3.1 rev.32
  55.4 3.5 copy.20
  58.9 3.1 rev.33
  62.0 3.5 copy.21
  65.5 3.1 rev.34
  68.6 2.2 copy.42
  70.8 1.9 copy.22
  72.7 3.1 rev.35
  75.8 1.9 constant_dynamic-update-slice_fusion.6
  77.7 1.9 constant_dynamic-update-slice_fusion.5
  79.7 1.9 constant_dynamic-update-slice_fusion.4
  81.6 1.9 constant_dynamic-update-slice_fusion.3
  83.5 0.0 copy-done.2
  83.5 0.3 constant_dynamic-update-slice_fusion.2
  83.8 0.0 copy-start.3
  83.8 5.2 copy-done.3
  89.1 93.3 %collective-permute-done = bf16[512,2048]{0,1:T(8,128)(2,1)} collective-permute-done((bf16[512,2048]{0,1:T(8,128)(2,1)}, bf16[512,2048]{0,1:T(8,128)(2,1)}, u32[]{:S(2)}, u32[]{:S(2)}) %collective-permute-start) | collective-permute-done | bytes 2097184 | tf_op jit(solution)/shard_map/ppermute | solution.py:19
  182.4 4.2 copy.26
  186.6 0.0 collective-permute-done.1
  186.6 3.9 copy.27
  190.5 3.4 constant_dynamic-update-slice_fusion.1
  194.0 3.4 constant_dynamic-update-slice_fusion
  197.4 2.7 reduce_sum.9
  200.1 112.8 %all-gather.5.cloned.1.call-done = bf16[7,16,128,1024]{3,2,0,1:T(8,128)(2,1)} async-done(((bf16[7,16,16,1024]{3,2,0,1:T(8,128)(2,1)}), bf16[7,16,128,1024]{3,2,0,1:T(8,128)(2,1)}) %all-gather.5.cloned.1.call-update) | async-done | bytes 29360144 | tf_op jit(solution)/shard_map/all_gather | solution.py:51
  312.9 31.9 %convolution_bitcast_fusion = f32[512,16,1024]{2,0,1:T(8,128)} fusion(bf16[7,512,16,128]{3,1,0,2:T(8,128)(2,1)} %constant_dynamic-update-slice_fusion, bf16[7,16,128,1024]{3,2,0,1:T(8,128)(2,1)} %all-gather.5.cloned.1.call-done), kind=kOutput, calls=%fused_computation.21 | convolution fusion | flops 15032385536 | bytes 77594624 | tf_op jit(solution)/shard_map/tabk,tbkn->abn/dot_general | solution.py:52
  344.9 32.4 %copy.29 = f32[512,16,1024]{0,2,1:T(8,128)} copy(f32[512,16,1024]{2,0,1:T(8,128)} %convolution_bitcast_fusion) | data formatting | bytes 67108864 | tf_op jit(solution)/shard_map/tabk,tbkn->abn/transpose | solution.py:52
  377.3 45.3 %copy.30 = f32[512,16384]{1,0:T(8,128)} copy(f32[512,16384]{0,1:T(8,128)} %bitcast.70) | data formatting | bytes 67108864 | tf_op jit(solution)/shard_map/reshape | solution.py:57
  422.6 82.0 %fusion.2 = bf16[512,16384]{1,0:T(8,128)(2,1)S(1)} fusion(f32[512,16384]{1,0:T(8,128)} %copy.30, bf16[512,16384]{1,0:T(8,128)(2,1)} %param.10, bf16[512,512]{1,0:T(8,128)(2,1)S(1)} %reduce_sum.9), kind=kOutput, calls=%fused_computation.3 | convolution fusion | flops 9143582720 | bytes 67633152 | tf_op jit(solution)/shard_map/dot_general | solution.py:59
  504.6 5.7 copy-done.1
  510.3 12.0 %copy.43 = bf16[64,8,16,1024]{3,2,1,0:T(8,128)(2,1)} copy(bf16[64,8,16,1024]{3,1,2,0:T(8,128)(2,1)S(1)} %bitcast.76) | data formatting | bytes 33554432
  522.3 91.5 %fusion.12 = f32[7,512,16,128]{1,3,0,2:T(8,128)} fusion(bf16[7,16,1024,128]{2,3,0,1:T(8,128)(2,1)} %all-gather.7.cloned.1.call-done, bf16[512,16,1024,1]{2,1,0,3:T(8,128)(2,1)} %bitcast.77), kind=kOutput, calls=%fused_computation.22 | convolution fusion | flops 15032385536 | bytes 75497472 | tf_op jit(solution)/shard_map/abn,tbnk->tabk/dot_general | solution.py:62
  613.8 17.7 %fusion.24 = (f32[1,512,16,128]{1,3,0,2:T(8,128)}, f32[512,16,128]{0,2,1:T(8,128)}, f32[1,512,16,128]{1,3,0,2:T(8,128)}, f32[1,512,16,128]{1,3,0,2:T(8,128)}, f3...) fusion(f32[7,512,16,128]{1,3,0,2:T(8,128)} %fusion.12), kind=kLoop, calls=%fused_computation.43 | loop fusion | bytes 50331648 | tf_op jit(solution)/shard_map/slice | solution.py:71
  631.5 1.3 collective-permute-start.2
  632.8 2.4 collective-permute-start.3
  635.2 4.8 rev.36
  639.9 4.7 rev.37
  644.6 4.7 rev.38
  649.4 4.8 rev.39
  654.2 18.1 %fusion.26 = f32[512,512]{1,0:T(8,128)} fusion(bf16[512,16384]{1,0:T(8,128)(2,1)} %copy-done.1, bf16[16384,512]{1,0:T(8,128)(2,1)} %param.12), kind=kOutput, calls=%fused_computation.45 | convolution fusion | flops 8589934592 | bytes 34603008 | tf_op jit(solution)/shard_map/dot_general | solution.py:76
  672.3 181.7 %all-reduce.1 = bf16[512,512]{1,0:T(8,128)(2,1)S(1)} all-reduce(f32[512,512]{1,0:T(8,128)} %fusion.26), channel_id=1, replica_groups=mesh['dp'=8,'hid'=4] {'hid'}, use_global_device_ids=true, to_apply=%region_1.2 | all-reduce | flops 262144 | bytes 1572864 | tf_op jit(solution)/shard_map/psum | solution.py:75
  854.0 3.2 fusion.27
  857.2 0.0 collective-permute-done.2
  857.2 0.0 collective-permute-done.3
  857.2 13.4 %fusion.20 = f32[512,16,128]{0,2,1:T(8,128)} fusion(f32[512,16,128]{0,2,1:T(8,128)} %collective-permute-done.3, f32[512,16,128]{0,2,1:T(8,128)} %collective-permute-done.2, f32[7,512,16,128]{1,3,0,2:T(8,128)} %fusion.12, f32[512,1,2,8,128]{0,4,3,2,1:T(8,128)} %rev.39, f32[512,2,2,4,128]{0,4,3,2,1:T(8,128)} %rev.38, f32[512,4,2,2,128]{0,4,3,2,1:T(8,128)} %rev.37, ...), kind=kLoop, calls=%fused_computation.31 | loop fusion | flops 6291456 | bytes 33554432 | tf_op jit(solution)/shard_map/add | solution.py:74
  870.5 5.4 copy.35
  875.9 5.4 add_convert_fusion
  (5 shorter events, 0.0 us)
Async XLA Ops:
  6.5 847.4 %copy-start = (bf16[512,2048]{1,0:T(8,128)(2,1)S(1)}, bf16[512,2048]{1,0:T(8,128)(2,1)}, u32[]{:S(2)}) copy-start(bf16[512,2048]{1,0:T(8,128)(2,1)} %param.13) | copy-start | bytes 6291460
  6.5 190.8 %all-gather.9.cloned.1.call-start = ((), (), s32[]{:S(2)}) async-start(), calls=%async_computation.2 | async-start | bytes 5242880 | tf_op jit(solution)/shard_map/all_gather | solution.py:8
  11.2 301.8 %all-gather.5.cloned.1.call-start = ((), (), s32[]{:S(2)}) async-start(), calls=%async_computation | async-start | bytes 33030144 | tf_op jit(solution)/shard_map/all_gather | solution.py:51
  15.8 506.5 %all-gather.7.cloned.1.call-start = ((), (), s32[]{:S(2)}) async-start(), calls=%async_computation.1 | async-start | bytes 33030144 | tf_op jit(solution)/shard_map/all_gather | solution.py:53
  26.0 156.4 %collective-permute-start = (bf16[512,2048]{0,1:T(8,128)(2,1)}, bf16[512,2048]{0,1:T(8,128)(2,1)}, u32[]{:S(2)}, u32[]{:S(2)}) collective-permute-start(bf16[512,2048]{0,1:T(8,128)(2,1)} %copy.18), channel_id=1, source_target_pairs={{0,1},{1,0},{2,3},{3,2},{4,5},{5,4},{6,7},{7,6},{8,9},{9,8},{10,11... | collective-permute-start | bytes 6291464 | tf_op jit(solution)/shard_map/ppermute | solution.py:19
  29.0 157.6 %collective-permute-start.1 = (bf16[512,2048]{0,1:T(8,128)(2,1)}, bf16[512,2048]{0,1:T(8,128)(2,1)}, u32[]{:S(2)}, u32[]{:S(2)}) collective-permute-start(bf16[512,2048]{0,1:T(8,128)(2,1)} %copy.18), channel_id=1, source_target_pairs={{0,2},{2,0},{1,3},{3,1},{4,6},{6,4},{5,7},{7,5},{8,10},{10,8},{9,1... | collective-permute-start | bytes 6291464 | tf_op jit(solution)/shard_map/ppermute | solution.py:19
  75.8 7.7 copy-start.2
  83.8 5.3 copy-start.3
  504.6 5.7 copy-start.1
  631.5 225.7 %collective-permute-start.2 = (f32[512,16,128]{0,2,1:T(8,128)}, f32[512,16,128]{0,2,1:T(8,128)}, u32[]{:S(2)}, u32[]{:S(2)}) collective-permute-start(f32[512,16,128]{0,2,1:T(8,128)} %get-tuple-element.10), channel_id=1, source_target_pairs={{0,1},{1,0},{2,3},{3,2},{4,5},{5,4},{6,7},{7,6},{8,9},{9,8},{10,11... | collective-permute-start | bytes 12582920 | tf_op jit(solution)/shard_map/ppermute | solution.py:19
  632.8 224.4 %collective-permute-start.3 = (f32[512,16,128]{0,2,1:T(8,128)}, f32[512,16,128]{0,2,1:T(8,128)}, u32[]{:S(2)}, u32[]{:S(2)}) collective-permute-start(f32[512,16,128]{0,2,1:T(8,128)} %get-tuple-element.6), channel_id=1, source_target_pairs={{0,2},{2,0},{1,3},{3,1},{4,6},{6,4},{5,7},{7,5},{8,10},{10,8},{9,1... | collective-permute-start | bytes 12582920 | tf_op jit(solution)/shard_map/ppermute | solution.py:19
Sparse Core Ops, SparseCore 0:
  11.3 155.9 all-gather.8
  169.2 143.7 all-gather.4
  314.8 148.8 all-gather.6
